TPU v7x, 32 devices: a whole 2x2x4 slice. The times are simulated.
32 devices in a mesh: parts: 2 (over y), tensor: 16 (over z, x, core).
Axes of the slice: x: 2, y: 2, z: 4, core: 2. Of those that a mesh axis runs over, the one named last changes fastest.
Arguments:
- cotangent: bfloat16 [384, 8192], P(('parts', 'tensor')), parts along dimension 0, may hold values from -6 to 6
- hidden: bfloat16 [384, 28672], P('parts', 'tensor'), parts along dimension 0, may hold values from -6 to 6
- down_weight: bfloat16 [28672, 8192], P('tensor'), may hold values from -0.0625 to 0.0625
- adapter_in: bfloat16 [28672, 2560], P('tensor'), may hold values from -0.119628906 to 0.119628906
- adapter_out: bfloat16 [2560, 8192], P(None, 'tensor'), may hold values from -0.0625 to 0.0625
- segment_ids: int32 [384], P('parts'), parts along dimension 0, may hold values from 0 to 11, never falling along the last dimension, each value on 1 to 32 neighbouring positions
- segment_dirs: int32 [24], P('parts'), parts along dimension 0, may hold values from 0 to 39
Outputs:
- grad_hidden: bfloat16 [384, 28672], P('parts', 'tensor'), parts along dimension 0
- grad_in: float32 [57344, 2560], P(('parts', 'tensor')), parts along dimension 0
- grad_out: float32 [5120, 8192], P('parts', 'tensor'), parts along dimension 0
There are 2 independent parts, one for each index of `parts`. A program takes and returns all parts, laid end to end along the dimension named above; an argument that names none is the same for every part. Nothing has to cross between parts.
Inputs may be any that keep to these rules, and one draw needn't show every extreme that they name: `segment_ids`: segment numbers never fall along the tokens; each segment holds 1 to 32 tokens.
All inputs are finite; a program needn't handle non-finite values.
Results may differ from a plain program's by a relative error of at most 0.005.
Values may be sent and summed in bfloat16 or wider, within the bound.
A program may use at most 192 MiB of HBM per device.

v0:
```python
import jax
import jax.numpy as jnp
from jax import lax
from jax.sharding import PartitionSpec as P

RANK = 64
NUM_DIR = 40


def direction_table(segment_ids, segment_dirs):
    seg_hot = (
        segment_ids[:, None] == jnp.arange(segment_dirs.shape[0], dtype=jnp.int32)[None, :]
    ).astype(jnp.float32)
    dir_hot = (segment_dirs[:, None] == jnp.arange(NUM_DIR, dtype=jnp.int32)[None, :]).astype(
        jnp.float32
    )
    return jnp.dot(seg_hot, dir_hot, precision=lax.Precision.HIGHEST)


def select_rank(wide, onehot):
    count = wide.shape[0]
    return jnp.sum(wide.reshape(count, NUM_DIR, RANK) * onehot[:, :, None], axis=1)


def spread_rank(low, onehot):
    count = low.shape[0]
    return (
        (0.5 * onehot[:, :, None] * low[:, None, :])
        .reshape(count, NUM_DIR * RANK)
        .astype(jnp.bfloat16)
    )


def low_sums(columns, hidden, adapter_in, adapter_out, onehot):
    wide_u = lax.dot_general(
        columns, adapter_out, (((1,), (1,)), ((), ())), preferred_element_type=jnp.float32
    )
    wide_v = jnp.dot(hidden, adapter_in, preferred_element_type=jnp.float32)
    part_u = select_rank(wide_u, onehot)
    part_v = select_rank(wide_v, onehot)
    return lax.psum((part_u, part_v), "tensor")


def rows_product(rows, spread_rows, down_weight, adapter_in):
    base = lax.dot_general(
        rows, down_weight, (((1,), (1,)), ((), ())), preferred_element_type=jnp.float32
    )
    extra = lax.dot_general(
        spread_rows, adapter_in, (((1,), (1,)), ((), ())), preferred_element_type=jnp.float32
    )
    return (base + extra).astype(jnp.bfloat16)


def per_device(cotangent, hidden, down_weight, adapter_in, adapter_out, segment_ids, segment_dirs):
    onehot = direction_table(segment_ids, segment_dirs)
    width_share = adapter_out.shape[1]
    full_rows = lax.all_gather(cotangent, "tensor", axis=0, tiled=True)
    columns = lax.dynamic_slice_in_dim(
        full_rows, lax.axis_index("tensor") * width_share, width_share, 1
    )
    low_u, low_v = low_sums(columns, hidden, adapter_in, adapter_out, onehot)
    spread_u = spread_rank(low_u, onehot)
    grad_hidden = rows_product(full_rows, spread_u, down_weight, adapter_in)
    spread_v = spread_rank(low_v, onehot)
    grad_in = lax.dot_general(
        hidden, spread_u, (((0,), (0,)), ((), ())), preferred_element_type=jnp.float32
    )
    grad_out = lax.dot_general(
        spread_v, columns, (((0,), (0,)), ((), ())), preferred_element_type=jnp.float32
    )
    return (grad_hidden, grad_in, grad_out)


def solution(mesh):
    return jax.shard_map(
        per_device,
        mesh=mesh,
        in_specs=(
            P(("parts", "tensor"), None),
            P("parts", "tensor"),
            P("tensor", None),
            P("tensor", None),
            P(None, "tensor"),
            P("parts"),
            P("parts"),
        ),
        out_specs=(P("parts", "tensor"), P(("parts", "tensor"), None), P("parts", "tensor")),
        check_vma=False,
    )
```

profile of v0, /device:TPU:0, one launch (start us, length us, event | category | flops | bytes accessed | tf_op | source)
XLA Modules:
  0.0 205.0 jit_solution(15566793694941472016)
XLA Ops:
  7.2 0.0 copy-start
  7.2 0.0 all-gather.3.cloned.1.call-start
  7.2 0.7 all-gather.3.cloned.1.call-update
  7.9 0.0 all-reduce.3.cloned.1.call-start
  8.0 0.9 broadcast_multiply_fusion
  8.9 9.0 %fusion.11 = f32[192,2560]{0,1:T(8,128)} fusion(bf16[192,1792]{1,0:T(8,128)(2,1)} %param.8, bf16[1792,2560]{1,0:T(8,128)(2,1)} %param.10), kind=kOutput, calls=%fused_computation.20 | convolution fusion | flops 1761607680 | bytes 11829248 | tf_op jit(solution)/shard_map/dot_general | solution.py:38
  17.9 45.3 %all-gather.3.cloned.1.call-done = bf16[16,12,8192]{2,1,0:T(8,128)(2,1)} async-done(((bf16[1,12,8192]{2,1,0:T(8,128)(2,1)}), bf16[16,12,8192]{2,1,0:T(8,128)(2,1)}) %all-gather.3.cloned.1.call-update) | async-done | bytes 3145744 | tf_op jit(solution)/shard_map/all_gather | solution.py:57
  63.3 4.7 %reshape.32 = bf16[192,8192]{1,0:T(8,128)(2,1)} reshape(bf16[16,12,8192]{2,1,0:T(8,128)(2,1)} %all-gather.3.cloned.1.call-done) | data formatting | bytes 6291456
  67.9 0.0 copy-done
  67.9 0.0 copy-start.2
  67.9 1.9 fusion.3
  69.9 0.0 copy-done.2
  69.9 1.3 multiply_reduce_fusion
  71.2 0.0 all-reduce.3.cloned.1.call-update
  71.2 16.1 %fusion.10 = f32[192,1792]{1,0:T(8,128)} fusion(bf16[192,8192]{1,0:T(8,128)(2,1)} %reshape.32, bf16[1792,8192]{1,0:T(8,128)(2,1)} %param.9), kind=kOutput, calls=%fused_computation.19 | convolution fusion | flops 5637144576 | bytes 33882112 | tf_op jit(solution)/shard_map/dot_general | solution.py:45
  87.3 0.0 copy-start.3
  87.3 71.0 %all-reduce.3.cloned.1.call-done = (f32[192,64]{0,1:T(8,128)}, f32[192,64]{0,1:T(8,128)}) async-done(((f32[192,64]{0,1:T(8,128)}, f32[192,64]{0,1:T(8,128)}), (f32[192,64]{0,1:T(8,128)}, f32[192,64]{0,1:T(8,128)})) %all-reduce.3.cloned.1.call-update) | async-done | bytes 98320 | tf_op jit(solution)/shard_map/psum | solution.py:41
  158.3 0.0 slice-start
  158.3 3.0 %multiply_convert_fusion = (bf16[192,40,64]{0,2,1:T(8,128)(2,1)}, bf16[192,40,64]{0,2,1:T(8,128)(2,1)S(1)}) fusion(f32[192,64]{0,1:T(8,128)} %get-tuple-element.15, f32[192,40]{0,1:T(8,128)S(1)} %get-tuple-element.18, f32[192,64]{0,1:T(8,128)} %get-tuple-element.14), kind=kLoop, calls=%fused_computation.1 | loop fusion | flops 1966080 | bytes 2095104 | tf_op jit(solution)/shard_map/convert_element_type | solution.py:30
  161.3 0.0 copy-done.3
  161.3 0.0 slice-start.1
  161.3 0.0 slice-start.2
  161.3 0.0 copy-start.4
  161.3 8.8 %convolution_bitcast_fusion = f32[1792,2560]{0,1:T(8,128)} fusion(bf16[192,2560]{0,1:T(8,128)(2,1)S(1)} %bitcast.19, bf16[192,1792]{1,0:T(8,128)(2,1)S(1)} %copy-done.3), kind=kOutput, calls=%fused_computation | convolution fusion | flops 1761607680 | bytes 20021248 | tf_op jit(solution)/shard_map/dot_general | solution.py:65
  170.1 0.0 slice-done
  170.1 0.0 slice-done.1
  170.2 0.0 slice-done.2
  170.2 0.0 copy-done.4
  170.2 4.1 %fusion = bf16[192,1792]{1,0:T(8,128)(2,1)} fusion(f32[192,1792]{1,0:T(8,128)S(1)} %copy-done.4, bf16[192,2560]{0,1:T(8,128)(2,1)S(1)} %bitcast.20, bf16[1792,2560]{1,0:T(8,128)(2,1)S(1)} %bitcast.24), kind=kOutput, calls=%fused_computation.6 | convolution fusion | flops 1762295808 | bytes 12222464 | tf_op jit(solution)/shard_map/dot_general | solution.py:48
  174.2 19.2 %copy.18 = f32[1792,2560]{1,0:T(8,128)} copy(f32[1792,2560]{0,1:T(8,128)} %convolution_bitcast_fusion) | data formatting | bytes 36700160
  193.5 0.0 copy-start.1
  193.5 4.7 %fusion.1 = f32[2560,512]{1,0:T(8,128)} fusion(bf16[192,2560]{0,1:T(8,128)(2,1)} %bitcast.18, bf16[192,8192]{1,0:T(8,128)(2,1)} %reshape.32, s32[]{:T(128)S(6)} %select_n.3), kind=kOutput, calls=%fused_computation.7 | convolution fusion | flops 503316480 | bytes 6750212 | tf_op jit(solution)/shard_map/dot_general | solution.py:68
  198.1 0.0 copy-done.1
  (1 shorter events, 0.0 us)
Async XLA Ops:
  7.2 60.8 %copy-start = (bf16[2560,512]{1,0:T(8,128)(2,1)S(1)}, bf16[2560,512]{1,0:T(8,128)(2,1)}, u32[]{:S(2)}) copy-start(bf16[2560,512]{1,0:T(8,128)(2,1)} %param.11) | copy-start | bytes 7864324
  7.2 56.1 %all-gather.3.cloned.1.call-start = ((), (), s32[]{:S(2)}) async-start(), calls=%async_computation | async-start | bytes 4456448 | tf_op jit(solution)/shard_map/all_gather | solution.py:57
  7.9 150.4 %all-reduce.3.cloned.1.call-start = ((), (), s32[]{:S(2)}) async-start(), calls=%async_computation.1 | async-start | bytes 262144 | tf_op jit(solution)/shard_map/psum | solution.py:41
  67.9 1.9 copy-start.2
  87.3 74.0 %copy-start.3 = (bf16[192,1792]{1,0:T(8,128)(2,1)S(1)}, bf16[192,1792]{1,0:T(8,128)(2,1)}, u32[]{:S(2)}) copy-start(bf16[192,1792]{1,0:T(8,128)(2,1)} %param.8) | copy-start | bytes 2064388
  158.3 11.8 %slice-start = ((s8[9175040]{0:T(1024)(128)(4,1)}), s8[4194304]{0:T(1024)(128)(4,1)S(1)}, s32[]{:S(2)}) async-start(s8[9175040]{0:T(1024)(128)(4,1)} %bitcast.23), calls=%async_computation.2 | async-start | bytes 8388608
  161.3 8.8 %slice-start.1 = ((s8[9175040]{0:T(1024)(128)(4,1)}), s8[4194304]{0:T(1024)(128)(4,1)S(1)}, s32[]{:S(2)}) async-start(s8[9175040]{0:T(1024)(128)(4,1)} %bitcast.23), calls=%async_computation.3 | async-start | bytes 8388608
  161.3 8.8 %slice-start.2 = ((s8[9175040]{0:T(1024)(128)(4,1)}), s8[786432]{0:T(1024)(128)(4,1)S(1)}, s32[]{:S(2)}) async-start(s8[9175040]{0:T(1024)(128)(4,1)} %bitcast.23), calls=%async_computation.4 | async-start | bytes 1572864
  161.3 8.8 %copy-start.4 = (f32[192,1792]{1,0:T(8,128)S(1)}, f32[192,1792]{1,0:T(8,128)}, u32[]{:S(2)}) copy-start(f32[192,1792]{1,0:T(8,128)} %fusion.10) | copy-start | bytes 4128772
  193.5 4.7 %copy-start.1 = (bf16[2560,512]{1,0:T(8,128)(2,1)S(1)}, bf16[2560,512]{1,0:T(8,128)(2,1)}, u32[]{:S(2)}) copy-start(bf16[2560,512]{1,0:T(8,128)(2,1)} %param.11) | copy-start | bytes 7864324
Sparse Core Ops, SparseCore 0:
  10.2 53.0 all-gather.2
  71.3 86.9 all-reduce.2
where the time goes:
time: 207 us; the launch traced here: 205 us
  waiting for transfers between devices  117 us (57%)
  matrix products  45.5 us (22%)
  local copies, waits for them, and re-layouts  24 us (12%)
  between operations  14.1 us (7%)
  other arithmetic  4.27 us (2%)
    psum x1, waiting for transfers between devices, low_sums(): return lax.psum((part_u, part_v), 'tensor')  71 us
    all_gather x1, waiting for transfers between devices, per_device(): full_rows = lax.all_gather(cotangent, 'tensor', axis=0, tiled=True)  45.3 us
    unnamed x18, local copies, waits for them, and re-layouts  24 us
    dot_general x1, matrix products, rows_product(): lax.dot_general(rows, down_weight, (((1,), (1,)), ((), ())), preferred_el...  16.1 us
    dot_general x1, matrix products, low_sums(): wide_v = jnp.dot(hidden, adapter_in, preferred_element_type=jnp.float32)  9.01 us
    dot_general x1, matrix products, per_device(): lax.dot_general(hidden, spread_u, (((0,), (0,)), ((), ())), preferred_ele...  8.83 us
    dot_general x1, matrix products, per_device(): lax.dot_general(spread_v, columns, (((0,), (0,)), ((), ())), preferred_el...  4.66 us
  transfers between devices with their start and end apart: 2, of which 2 were waited for; matrix products, arithmetic and copies ran while one was open for 13% of the time, Pallas kernels for 0%

commit v1 on v0

--- a/solution.py
+++ b/solution.py
@@ -31,43 +31,50 @@
     )
 
 
-def low_sums(columns, hidden, adapter_in, adapter_out, onehot):
-    wide_u = lax.dot_general(
-        columns, adapter_out, (((1,), (1,)), ((), ())), preferred_element_type=jnp.float32
-    )
-    wide_v = jnp.dot(hidden, adapter_in, preferred_element_type=jnp.float32)
-    part_u = select_rank(wide_u, onehot)
-    part_v = select_rank(wide_v, onehot)
-    return lax.psum((part_u, part_v), "tensor")
+def gather_blocks(own, shards):
+    tiled = jnp.broadcast_to(own[None], (shards,) + own.shape)
+    got = lax.all_to_all(tiled, "tensor", 0, 0, tiled=True)
+    return got.reshape((shards * own.shape[0],) + own.shape[1:])
 
 
-def rows_product(rows, spread_rows, down_weight, adapter_in):
-    base = lax.dot_general(
-        rows, down_weight, (((1,), (1,)), ((), ())), preferred_element_type=jnp.float32
-    )
-    extra = lax.dot_general(
-        spread_rows, adapter_in, (((1,), (1,)), ((), ())), preferred_element_type=jnp.float32
-    )
-    return (base + extra).astype(jnp.bfloat16)
+def sum_blocks(partial, shards):
+    rows = partial.shape[0] // shards
+    pieces = partial.reshape((shards, rows) + partial.shape[1:])
+    got = lax.all_to_all(pieces, "tensor", 0, 0, tiled=True)
+    return gather_blocks(jnp.sum(got, axis=0), shards)
 
 
 def per_device(cotangent, hidden, down_weight, adapter_in, adapter_out, segment_ids, segment_dirs):
     onehot = direction_table(segment_ids, segment_dirs)
     width_share = adapter_out.shape[1]
+    shards = cotangent.shape[1] // width_share
+    own = cotangent.shape[0]
     full_rows = lax.all_gather(cotangent, "tensor", axis=0, tiled=True)
-    columns = lax.dynamic_slice_in_dim(
-        full_rows, lax.axis_index("tensor") * width_share, width_share, 1
+    pieces = cotangent.reshape(own, shards, width_share).transpose(1, 0, 2)
+    columns = lax.all_to_all(pieces, "tensor", 0, 0, tiled=True).reshape(
+        shards * own, width_share
     )
-    low_u, low_v = low_sums(columns, hidden, adapter_in, adapter_out, onehot)
-    spread_u = spread_rank(low_u, onehot)
-    grad_hidden = rows_product(full_rows, spread_u, down_weight, adapter_in)
-    spread_v = spread_rank(low_v, onehot)
+    wide_u = lax.dot_general(
+        columns, adapter_out, (((1,), (1,)), ((), ())), preferred_element_type=jnp.float32
+    )
+    wide_v = jnp.dot(hidden, adapter_in, preferred_element_type=jnp.float32)
+    part = jnp.concatenate([select_rank(wide_u, onehot), select_rank(wide_v, onehot)], axis=1)
+    low = sum_blocks(part, shards)
+    spread_u = spread_rank(low[:, :RANK], onehot)
+    spread_v = spread_rank(low[:, RANK:], onehot)
     grad_in = lax.dot_general(
         hidden, spread_u, (((0,), (0,)), ((), ())), preferred_element_type=jnp.float32
     )
     grad_out = lax.dot_general(
         spread_v, columns, (((0,), (0,)), ((), ())), preferred_element_type=jnp.float32
     )
+    extra = lax.dot_general(
+        spread_u, adapter_in, (((1,), (1,)), ((), ())), preferred_element_type=jnp.float32
+    )
+    base = lax.dot_general(
+        full_rows, down_weight, (((1,), (1,)), ((), ())), preferred_element_type=jnp.float32
+    )
+    grad_hidden = (base + extra).astype(jnp.bfloat16)
     return (grad_hidden, grad_in, grad_out)
 
 

time: 207 us -> 128 us (0.62)
  waiting for transfers between devices: 117 us -> 13.6 us
  blocking collectives: 0 us -> 12.9 us
  starting transfers between devices: 0.08 us -> 11.1 us
  other arithmetic: 4.27 us -> 1.26 us
  local copies, waits for them, and re-layouts: 24 us -> 27 us
    psum x1 -> x0, waiting for transfers between devices: 71 us -> none  [low_sums(): return lax.psum((part_u, part_v), 'tensor')]
    all_gather x1, waiting for transfers between devices: 45.3 us -> 0.01 us  [per_device(): full_rows = lax.all_gather(cotangent, 'tensor', axis=0, tiled=True)]
    all_to_all x0 -> x2, waiting for transfers between devices: none -> 12.9 us  [the longest x1 10.2 us: gather_blocks(): got = lax.all_to_all(tiled, 'tensor', 0, 0, tiled=True)]
    all_to_all x0 -> x1, blocking collectives: none -> 12.9 us  [sum_blocks(): got = lax.all_to_all(pieces, 'tensor', 0, 0, tiled=True)]
    all_to_all x0 -> x2, starting transfers between devices: none -> 11.1 us  [the longest x1 7.39 us: per_device(): lax.all_to_all(pieces, 'tensor', 0, 0, tiled=True)]
    dot_general x4, matrix products: 31.1 us -> 33.4 us  [the longest x1 16.9 us: per_device(): lax.dot_general(full_rows, down_weight, (((1,), (1,)), ((), ())), preferr...]
    convert_element_type x1, other arithmetic: 2.96 us -> 0.85 us  [spread_rank(): return (0.5 * onehot[:, :, None] * low[:, None, :]).reshape(count, NUM_DI...]
    unnamed x18 -> x15, local copies, waits for them, and re-layouts: 24 us -> 25 us
  transfers between devices with their start and end apart: 2 -> 3, of which waited for: 2 -> 2; matrix products, arithmetic and copies ran while one was open for 13% -> 36% of each run, Pallas kernels for 0% -> 0%
where the time goes in v1:
time: 128 us; the launch traced here: 127 us
  matrix products  47.3 us (37%)
  local copies, waits for them, and re-layouts  27 us (21%)
  between operations  14.2 us (11%)
  waiting for transfers between devices  13.6 us (11%)
  blocking collectives  12.9 us (10%)
  starting transfers between devices  11.1 us (9%)
    unnamed x15, local copies, waits for them, and re-layouts  25 us
    dot_general x1, matrix products, per_device(): lax.dot_general(full_rows, down_weight, (((1,), (1,)), ((), ())), preferr...  16.9 us
    all_to_all x1, blocking collectives, sum_blocks(): got = lax.all_to_all(pieces, 'tensor', 0, 0, tiled=True)  12.9 us
    dot_general x1, matrix products, per_device(): lax.dot_general(hidden, spread_u, (((0,), (0,)), ((), ())), preferred_ele...  10.4 us
    all_to_all x1, waiting for transfers between devices, gather_blocks(): got = lax.all_to_all(tiled, 'tensor', 0, 0, tiled=True)  10.2 us
    dot_general x1, matrix products, per_device(): wide_v = jnp.dot(hidden, adapter_in, preferred_element_type=jnp.float32)  7.84 us
    dot_general x1, matrix products, per_device(): lax.dot_general(spread_u, adapter_in, (((1,), (1,)), ((), ())), preferred...  7.8 us
    all_to_all x1, starting transfers between devices, per_device(): lax.all_to_all(pieces, 'tensor', 0, 0, tiled=True)  7.39 us
  transfers between devices with their start and end apart: 3, of which 2 were waited for; matrix products, arithmetic and copies ran while one was open for 36% of the time, Pallas kernels for 0%

profile of v1, /device:TPU:0, one launch (start us, length us, event | category | flops | bytes accessed | tf_op | source)
XLA Modules:
  0.0 127.3 jit_solution(7212833007659860789)
XLA Ops:
  7.2 0.0 copy-start
  7.2 0.0 all-gather.3.cloned.1.call-start
  7.2 0.7 all-gather.3.cloned.1.call-update
  7.9 1.1 copy.26
  9.0 0.8 copy.28
  9.8 7.4 %all-to-all-start = ((bf16[16,12,512]{2,1,0:T(8,128)(2,1)}), bf16[16,12,512]{2,1,0:T(8,128)(2,1)S(1)}, u32[]{:S(2)}, u32[]{:S(2)}) async-start(bf16[16,12,512]{2,1,0:T(8,128)(2,1)} %bitcast.24), calls=%async_computation | async-start | bytes 524288 | tf_op jit(solution)/shard_map/all_to_all | solution.py:54
  17.2 0.0 copy-start.4
  17.2 0.0 copy-start.5
  17.3 7.8 %fusion.6 = f32[192,2560]{0,1:T(8,128)S(1)} fusion(bf16[192,1792]{1,0:T(8,128)(2,1)} %param.8, bf16[1792,2560]{1,0:T(8,128)(2,1)} %param.10), kind=kOutput, calls=%fused_computation.17 | convolution fusion | flops 1761607680 | bytes 11829248 | tf_op jit(solution)/shard_map/dot_general | solution.py:60
  25.1 0.0 copy-done.4
  25.1 0.0 copy-done.5
  25.1 0.3 broadcast_multiply_fusion
  25.4 0.4 multiply_reduce_fusion
  25.8 2.7 %all-to-all-done = bf16[16,12,512]{2,1,0:T(8,128)(2,1)S(1)} async-done(((bf16[16,12,512]{2,1,0:T(8,128)(2,1)}), bf16[16,12,512]{2,1,0:T(8,128)(2,1)S(1)}, u32[]{:S(2)}, u32[]{:S(2)}) %all-to-all-start) | async-done | bytes 196640 | tf_op jit(solution)/shard_map/all_to_all | solution.py:54
  28.6 0.0 copy-done
  28.6 0.9 multiply_reduce_fusion.1
  29.5 0.1 copy.21
  29.6 12.9 %all_to_all.15 = f32[16,12,128]{2,1,0:T(8,128)S(1)} all-to-all(f32[16,12,128]{2,1,0:T(8,128)S(1)} %reshape.52), channel_id=1, replica_groups=mesh['parts'=2,'tensor'=16] {'tensor'}, dimensions={0} | all-to-all | bytes 196608 | tf_op jit(solution)/shard_map/all_to_all | solution.py:43
  42.5 0.7 broadcast_in_dim.2
  43.2 3.7 %all-to-all-start.2 = ((f32[16,12,128]{2,1,0:T(8,128)}), f32[16,12,128]{2,1,0:T(8,128)S(1)}, u32[]{:S(2)}, u32[]{:S(2)}) async-start(f32[16,12,128]{2,1,0:T(8,128)} %broadcast_in_dim.2), calls=%async_computation.2 | async-start | bytes 262144 | tf_op jit(solution)/shard_map/all_to_all | solution.py:36
  46.9 10.2 %all-to-all-done.2 = f32[16,12,128]{2,1,0:T(8,128)S(1)} async-done(((f32[16,12,128]{2,1,0:T(8,128)}), f32[16,12,128]{2,1,0:T(8,128)S(1)}, u32[]{:S(2)}, u32[]{:S(2)}) %all-to-all-start.2) | async-done | bytes 98336 | tf_op jit(solution)/shard_map/all_to_all | solution.py:36
  57.1 0.1 fusion.4
  57.2 0.1 copy.23
  57.3 0.1 copy.22
  57.4 0.8 multiply_convert_fusion
  58.2 0.0 copy-start.2
  58.2 10.4 %convolution_bitcast_fusion = f32[1792,2560]{0,1:T(8,128)} fusion(bf16[192,2560]{0,1:T(8,128)(2,1)S(1)} %bitcast.27, bf16[192,1792]{1,0:T(8,128)(2,1)} %param.8), kind=kOutput, calls=%fused_computation | convolution fusion | flops 1761607680 | bytes 20021248 | tf_op jit(solution)/shard_map/dot_general | solution.py:65
  68.7 0.0 copy-done.2
  68.7 19.2 %copy.24 = f32[1792,2560]{1,0:T(8,128)} copy(f32[1792,2560]{0,1:T(8,128)} %convolution_bitcast_fusion) | data formatting | bytes 36700160
  87.9 3.2 %fusion.7 = f32[2560,512]{1,0:T(8,128)} fusion(bf16[192,2560]{0,1:T(8,128)(2,1)S(1)} %bitcast.26, bf16[192,512]{1,0:T(8,128)(2,1)S(1)} %reshape.50), kind=kOutput, calls=%fused_computation.18 | convolution fusion | flops 503316480 | bytes 6422528 | tf_op jit(solution)/shard_map/dot_general | solution.py:68
  91.1 0.0 all-gather.3.cloned.1.call-done
  91.1 4.7 %reshape.55 = bf16[192,8192]{1,0:T(8,128)(2,1)} reshape(bf16[16,12,8192]{2,1,0:T(8,128)(2,1)} %all-gather.3.cloned.1.call-done) | data formatting | bytes 6291456
  95.8 0.0 copy-start.3
  95.8 16.9 %fusion.5 = f32[192,1792]{1,0:T(8,128)S(1)} fusion(bf16[192,8192]{1,0:T(8,128)(2,1)} %reshape.55, bf16[1792,8192]{1,0:T(8,128)(2,1)} %param.9), kind=kOutput, calls=%fused_computation.16 | convolution fusion | flops 5637144576 | bytes 33882112 | tf_op jit(solution)/shard_map/dot_general | solution.py:74
  112.7 0.0 copy-done.3
  112.7 0.0 copy-start.1
  112.7 7.8 %fusion = bf16[192,1792]{1,0:T(8,128)(2,1)} fusion(f32[192,1792]{1,0:T(8,128)S(1)} %fusion.5, bf16[192,2560]{0,1:T(8,128)(2,1)S(1)} %bitcast.28, bf16[1792,2560]{1,0:T(8,128)(2,1)} %param.10), kind=kOutput, calls=%fused_computation.6 | convolution fusion | flops 1762295808 | bytes 12222464 | tf_op jit(solution)/shard_map/dot_general | solution.py:71
  120.5 0.0 copy-done.1
  (7 shorter events, 0.2 us)
Async XLA Ops:
  7.2 21.4 %copy-start = (bf16[2560,512]{1,0:T(8,128)(2,1)S(1)}, bf16[2560,512]{1,0:T(8,128)(2,1)}, u32[]{:S(2)}) copy-start(bf16[2560,512]{1,0:T(8,128)(2,1)} %param.11) | copy-start | bytes 7864324
  7.2 83.9 %all-gather.3.cloned.1.call-start = ((), (), s32[]{:S(2)}) async-start(), calls=%async_computation.3 | async-start | bytes 4456448 | tf_op jit(solution)/shard_map/all_gather | solution.py:52
  9.8 18.7 %all-to-all-start = ((bf16[16,12,512]{2,1,0:T(8,128)(2,1)}), bf16[16,12,512]{2,1,0:T(8,128)(2,1)S(1)}, u32[]{:S(2)}, u32[]{:S(2)}) async-start(bf16[16,12,512]{2,1,0:T(8,128)(2,1)} %bitcast.24), calls=%async_computation | async-start | bytes 524288 | tf_op jit(solution)/shard_map/all_to_all | solution.py:54
  17.2 7.9 %copy-start.4 = (s32[192]{0:T(256)S(1)}, s32[192]{0:T(256)}, u32[]{:S(2)}) copy-start(s32[192]{0:T(256)} %param.12) | copy-start | bytes 2308
  17.2 7.9 %copy-start.5 = (s32[12]{0:T(128)S(1)}, s32[12]{0:T(128)}, u32[]{:S(2)}) copy-start(s32[12]{0:T(128)} %param.13) | copy-start | bytes 148
  43.2 13.9 %all-to-all-start.2 = ((f32[16,12,128]{2,1,0:T(8,128)}), f32[16,12,128]{2,1,0:T(8,128)S(1)}, u32[]{:S(2)}, u32[]{:S(2)}) async-start(f32[16,12,128]{2,1,0:T(8,128)} %broadcast_in_dim.2), calls=%async_computation.2 | async-start | bytes 262144 | tf_op jit(solution)/shard_map/all_to_all | solution.py:36
  58.2 10.4 %copy-start.2 = (bf16[192,40,64]{0,2,1:T(8,128)(2,1)}, bf16[192,40,64]{0,2,1:T(8,128)(2,1)S(1)}, u32[]{:S(2)}) copy-start(bf16[192,40,64]{0,2,1:T(8,128)(2,1)S(1)} %get-tuple-element.15) | copy-start | bytes 2949124
  95.8 16.9 %copy-start.3 = (bf16[192,40,64]{0,2,1:T(8,128)(2,1)S(1)}, bf16[192,40,64]{0,2,1:T(8,128)(2,1)}, u32[]{:S(2)}) copy-start(bf16[192,40,64]{0,2,1:T(8,128)(2,1)} %copy-done.2) | copy-start | bytes 2949124
  112.7 7.8 %copy-start.1 = (bf16[2560,512]{1,0:T(8,128)(2,1)S(1)}, bf16[2560,512]{1,0:T(8,128)(2,1)}, u32[]{:S(2)}) copy-start(bf16[2560,512]{1,0:T(8,128)(2,1)} %param.11) | copy-start | bytes 7864324
Sparse Core Ops, SparseCore 0:
  10.2 56.6 all-gather.2

commit v2 on v1

--- a/solution.py
+++ b/solution.py
@@ -1,6 +1,7 @@
 import jax
 import jax.numpy as jnp
 from jax import lax
+from jax.experimental import pallas as pl
 from jax.sharding import PartitionSpec as P
 
 RANK = 64
@@ -29,6 +30,26 @@
         .reshape(count, NUM_DIR * RANK)
         .astype(jnp.bfloat16)
     )
+
+
+def _rows_kernel(lhs_ref, rhs_ref, out_ref):
+    out_ref[...] = jnp.dot(lhs_ref[...], rhs_ref[...], preferred_element_type=jnp.float32)
+
+
+def rows_matmul(lhs, rhs):
+    m, k = lhs.shape
+    n = rhs.shape[1]
+    tile = next((t for t in (512, 256, 128) if m % t == 0), m)
+    return pl.pallas_call(
+        _rows_kernel,
+        grid=(m // tile,),
+        in_specs=[
+            pl.BlockSpec((tile, k), lambda i: (i, 0)),
+            pl.BlockSpec((k, n), lambda i: (0, 0)),
+        ],
+        out_specs=pl.BlockSpec((tile, n), lambda i: (i, 0)),
+        out_shape=jax.ShapeDtypeStruct((m, n), jnp.float32),
+    )(lhs, rhs)
 
 
 def gather_blocks(own, shards):
@@ -62,9 +83,7 @@
     low = sum_blocks(part, shards)
     spread_u = spread_rank(low[:, :RANK], onehot)
     spread_v = spread_rank(low[:, RANK:], onehot)
-    grad_in = lax.dot_general(
-        hidden, spread_u, (((0,), (0,)), ((), ())), preferred_element_type=jnp.float32
-    )
+    grad_in = rows_matmul(hidden.T, spread_u)
     grad_out = lax.dot_general(
         spread_v, columns, (((0,), (0,)), ((), ())), preferred_element_type=jnp.float32
     )

time: 128 us -> 109 us (0.85)
  local copies, waits for them, and re-layouts: 27 us -> 11.4 us
  matrix products: 47.3 us -> 36.8 us
  Pallas kernels: 0 us -> 9.34 us
  waiting for transfers between devices: 13.6 us -> 11.4 us
    unnamed x15, local copies, waits for them, and re-layouts: 25 us -> 8.02 us
    dot_general x1 -> x0, matrix products: 10.4 us -> none  [per_device(): lax.dot_general(hidden, spread_u, (((0,), (0,)), ((), ())), preferred_ele...]
    pallas_call x0 -> x1, Pallas kernels: none -> 9.34 us  [rows_matmul(): pl.pallas_call(_rows_kernel, grid=(m // tile,), in_specs=[pl.BlockSpec((t...]
    all_to_all x1, waiting for transfers between devices: 10.2 us -> 7.96 us  [gather_blocks(): got = lax.all_to_all(tiled, 'tensor', 0, 0, tiled=True)]
    convert_element_type x0 -> x1, local copies, waits for them, and re-layouts: none -> 1.43 us  [spread_rank(): return (0.5 * onehot[:, :, None] * low[:, None, :]).reshape(count, NUM_DI...]
  transfers between devices with their start and end apart: 3 -> 3, of which waited for: 2 -> 2; matrix products, arithmetic and copies ran while one was open for 36% -> 19% of each run, Pallas kernels for 0% -> 9%
where the time goes in v2:
time: 109 us; the launch traced here: 108 us
  matrix products  36.8 us (34%)
  between operations  14.2 us (13%)
  blocking collectives  12.9 us (12%)
  local copies, waits for them, and re-layouts  11.4 us (10%)
  waiting for transfers between devices  11.4 us (10%)
  starting transfers between devices  11.1 us (10%)
  Pallas kernels  9.34 us (9%)
  other arithmetic  1.26 us (1%)
    dot_general x1, matrix products, per_device(): lax.dot_general(full_rows, down_weight, (((1,), (1,)), ((), ())), preferr...  16.9 us
    all_to_all x1, blocking collectives, sum_blocks(): got = lax.all_to_all(pieces, 'tensor', 0, 0, tiled=True)  12.9 us
    pallas_call x1, Pallas kernels, rows_matmul(): pl.pallas_call(_rows_kernel, grid=(m // tile,), in_specs=[pl.BlockSpec((t...  9.34 us
    unnamed x15, local copies, waits for them, and re-layouts  8.02 us
    all_to_all x1, waiting for transfers between devices, gather_blocks(): got = lax.all_to_all(tiled, 'tensor', 0, 0, tiled=True)  7.96 us
    dot_general x1, matrix products, per_device(): wide_v = jnp.dot(hidden, adapter_in, preferred_element_type=jnp.float32)  7.84 us
    dot_general x1, matrix products, per_device(): lax.dot_general(spread_u, adapter_in, (((1,), (1,)), ((), ())), preferred...  7.8 us
    all_to_all x1, starting transfers between devices, per_device(): lax.all_to_all(pieces, 'tensor', 0, 0, tiled=True)  7.39 us
  transfers between devices with their start and end apart: 3, of which 2 were waited for; matrix products, arithmetic and copies ran while one was open for 19% of the time, Pallas kernels for 9%

profile of v2, /device:TPU:0, one launch (start us, length us, event | category | flops | bytes accessed | tf_op | source)
XLA Modules:
  0.0 108.4 jit_solution(3983815215349940512)
XLA Ops:
  7.2 0.0 copy-start
  7.2 0.0 all-gather.3.cloned.1.call-start
  7.2 0.7 all-gather.3.cloned.1.call-update
  7.9 1.1 copy.28
  9.0 0.8 copy.30
  9.8 7.4 %all-to-all-start = ((bf16[16,12,512]{2,1,0:T(8,128)(2,1)}), bf16[16,12,512]{2,1,0:T(8,128)(2,1)S(1)}, u32[]{:S(2)}, u32[]{:S(2)}) async-start(bf16[16,12,512]{2,1,0:T(8,128)(2,1)} %bitcast.21), calls=%async_computation | async-start | bytes 524288 | tf_op jit(solution)/shard_map/all_to_all | solution.py:75
  17.2 0.0 copy-start.4
  17.2 0.0 copy-start.5
  17.3 7.8 %fusion.6 = f32[192,2560]{0,1:T(8,128)S(1)} fusion(bf16[192,1792]{1,0:T(8,128)(2,1)} %param.8, bf16[1792,2560]{1,0:T(8,128)(2,1)} %param.10), kind=kOutput, calls=%fused_computation.16 | convolution fusion | flops 1761607680 | bytes 11829248 | tf_op jit(solution)/shard_map/dot_general | solution.py:81
  25.1 0.0 copy-done.4
  25.1 0.0 copy-done.5
  25.1 0.3 broadcast_multiply_fusion
  25.4 0.4 multiply_reduce_fusion
  25.8 2.7 %all-to-all-done = bf16[16,12,512]{2,1,0:T(8,128)(2,1)S(1)} async-done(((bf16[16,12,512]{2,1,0:T(8,128)(2,1)}), bf16[16,12,512]{2,1,0:T(8,128)(2,1)S(1)}, u32[]{:S(2)}, u32[]{:S(2)}) %all-to-all-start) | async-done | bytes 196640 | tf_op jit(solution)/shard_map/all_to_all | solution.py:75
  28.6 0.0 copy-done
  28.6 0.9 multiply_reduce_fusion.1
  29.5 0.1 copy.22
  29.6 12.9 %all_to_all.15 = f32[16,12,128]{2,1,0:T(8,128)S(1)} all-to-all(f32[16,12,128]{2,1,0:T(8,128)S(1)} %reshape.52), channel_id=1, replica_groups=mesh['parts'=2,'tensor'=16] {'tensor'}, dimensions={0} | all-to-all | bytes 196608 | tf_op jit(solution)/shard_map/all_to_all | solution.py:64
  42.5 0.7 broadcast_in_dim.2
  43.2 3.7 %all-to-all-start.2 = ((f32[16,12,128]{2,1,0:T(8,128)}), f32[16,12,128]{2,1,0:T(8,128)S(1)}, u32[]{:S(2)}, u32[]{:S(2)}) async-start(f32[16,12,128]{2,1,0:T(8,128)} %broadcast_in_dim.2), calls=%async_computation.2 | async-start | bytes 262144 | tf_op jit(solution)/shard_map/all_to_all | solution.py:57
  46.9 2.2 %copy.24 = bf16[192,1792]{0,1:T(8,128)(2,1)} copy(bf16[192,1792]{1,0:T(8,128)(2,1)} %param.8) | data formatting | bytes 1376256 | tf_op args[1]
  49.1 8.0 %all-to-all-done.2 = f32[16,12,128]{2,1,0:T(8,128)S(1)} async-done(((f32[16,12,128]{2,1,0:T(8,128)}), f32[16,12,128]{2,1,0:T(8,128)S(1)}, u32[]{:S(2)}, u32[]{:S(2)}) %all-to-all-start.2) | async-done | bytes 98336 | tf_op jit(solution)/shard_map/all_to_all | solution.py:57
  57.1 0.1 fusion.4
  57.2 0.1 copy.26
  57.3 0.1 copy.23
  57.4 0.8 multiply_convert_fusion
  58.2 0.0 copy-start.2
  58.2 1.4 %copy.25.rhs_ref = bf16[192,2560]{1,0:T(8,128)(2,1)} copy(bf16[192,2560]{0,1:T(8,128)(2,1)S(1)} %bitcast.24) | data formatting | bytes 1966080 | tf_op jit(solution)/shard_map/convert_element_type | solution.py:31
  59.6 9.3 %shard_map.94 = f32[1792,2560]{1,0:T(8,128)} custom-call(bf16[1792,192]{1,0:T(8,128)(2,1)} %bitcast.26, bf16[192,2560]{1,0:T(8,128)(2,1)} %copy.25.rhs_ref), custom_call_target="tpu_custom_call" | custom-call | tf_op jit(solution)/shard_map/pallas_call | solution.py:43
  69.0 0.0 copy-done.2
  69.0 3.2 %fusion.7 = f32[2560,512]{1,0:T(8,128)} fusion(bf16[192,2560]{0,1:T(8,128)(2,1)S(1)} %bitcast.23, bf16[192,512]{1,0:T(8,128)(2,1)S(1)} %reshape.50), kind=kOutput, calls=%fused_computation.17 | convolution fusion | flops 503316480 | bytes 6422528 | tf_op jit(solution)/shard_map/dot_general | solution.py:87
  72.2 0.0 all-gather.3.cloned.1.call-done
  72.2 4.7 %reshape.55 = bf16[192,8192]{1,0:T(8,128)(2,1)} reshape(bf16[16,12,8192]{2,1,0:T(8,128)(2,1)} %all-gather.3.cloned.1.call-done) | data formatting | bytes 6291456
  76.9 0.0 copy-start.3
  76.9 16.9 %fusion.5 = f32[192,1792]{1,0:T(8,128)S(1)} fusion(bf16[192,8192]{1,0:T(8,128)(2,1)} %reshape.55, bf16[1792,8192]{1,0:T(8,128)(2,1)} %param.9), kind=kOutput, calls=%fused_computation.15 | convolution fusion | flops 5637144576 | bytes 33882112 | tf_op jit(solution)/shard_map/dot_general | solution.py:93
  93.8 0.0 copy-done.3
  93.8 0.0 copy-start.1
  93.8 7.8 %fusion = bf16[192,1792]{1,0:T(8,128)(2,1)} fusion(f32[192,1792]{1,0:T(8,128)S(1)} %fusion.5, bf16[192,2560]{0,1:T(8,128)(2,1)S(1)} %bitcast.25, bf16[1792,2560]{1,0:T(8,128)(2,1)} %param.10), kind=kOutput, calls=%fused_computation.5 | convolution fusion | flops 1762295808 | bytes 12222464 | tf_op jit(solution)/shard_map/dot_general | solution.py:90
  101.6 0.0 copy-done.1
  (7 shorter events, 0.2 us)
Async XLA Ops:
  7.2 21.4 %copy-start = (bf16[2560,512]{1,0:T(8,128)(2,1)S(1)}, bf16[2560,512]{1,0:T(8,128)(2,1)}, u32[]{:S(2)}) copy-start(bf16[2560,512]{1,0:T(8,128)(2,1)} %param.11) | copy-start | bytes 7864324
  7.2 65.0 %all-gather.3.cloned.1.call-start = ((), (), s32[]{:S(2)}) async-start(), calls=%async_computation.3 | async-start | bytes 4456448 | tf_op jit(solution)/shard_map/all_gather | solution.py:73
  9.8 18.7 %all-to-all-start = ((bf16[16,12,512]{2,1,0:T(8,128)(2,1)}), bf16[16,12,512]{2,1,0:T(8,128)(2,1)S(1)}, u32[]{:S(2)}, u32[]{:S(2)}) async-start(bf16[16,12,512]{2,1,0:T(8,128)(2,1)} %bitcast.21), calls=%async_computation | async-start | bytes 524288 | tf_op jit(solution)/shard_map/all_to_all | solution.py:75
  17.2 7.9 %copy-start.4 = (s32[192]{0:T(256)S(1)}, s32[192]{0:T(256)}, u32[]{:S(2)}) copy-start(s32[192]{0:T(256)} %param.12) | copy-start | bytes 2308
  17.2 7.9 %copy-start.5 = (s32[12]{0:T(128)S(1)}, s32[12]{0:T(128)}, u32[]{:S(2)}) copy-start(s32[12]{0:T(128)} %param.13) | copy-start | bytes 148
  43.2 13.9 %all-to-all-start.2 = ((f32[16,12,128]{2,1,0:T(8,128)}), f32[16,12,128]{2,1,0:T(8,128)S(1)}, u32[]{:S(2)}, u32[]{:S(2)}) async-start(f32[16,12,128]{2,1,0:T(8,128)} %broadcast_in_dim.2), calls=%async_computation.2 | async-start | bytes 262144 | tf_op jit(solution)/shard_map/all_to_all | solution.py:57
  58.2 10.8 %copy-start.2 = (bf16[192,40,64]{0,2,1:T(8,128)(2,1)}, bf16[192,40,64]{0,2,1:T(8,128)(2,1)S(1)}, u32[]{:S(2)}) copy-start(bf16[192,40,64]{0,2,1:T(8,128)(2,1)S(1)} %get-tuple-element.6) | copy-start | bytes 2949124
  76.9 16.9 %copy-start.3 = (bf16[192,40,64]{0,2,1:T(8,128)(2,1)S(1)}, bf16[192,40,64]{0,2,1:T(8,128)(2,1)}, u32[]{:S(2)}) copy-start(bf16[192,40,64]{0,2,1:T(8,128)(2,1)} %copy-done.2) | copy-start | bytes 2949124
  93.8 7.8 %copy-start.1 = (bf16[2560,512]{1,0:T(8,128)(2,1)S(1)}, bf16[2560,512]{1,0:T(8,128)(2,1)}, u32[]{:S(2)}) copy-start(bf16[2560,512]{1,0:T(8,128)(2,1)} %param.11) | copy-start | bytes 7864324
Sparse Core Ops, SparseCore 0:
  10.1 56.6 all-gather.2

commit v3 on v2

--- a/solution.py
+++ b/solution.py
@@ -59,6 +59,9 @@
 
 
 def sum_blocks(partial, shards):
+    if shards <= 16:
+        tiled = jnp.broadcast_to(partial[None], (shards,) + partial.shape)
+        return jnp.sum(lax.all_to_all(tiled, "tensor", 0, 0, tiled=True), axis=0)
     rows = partial.shape[0] // shards
     pieces = partial.reshape((shards, rows) + partial.shape[1:])
     got = lax.all_to_all(pieces, "tensor", 0, 0, tiled=True)
@@ -87,8 +90,10 @@
     grad_out = lax.dot_general(
         spread_v, columns, (((0,), (0,)), ((), ())), preferred_element_type=jnp.float32
     )
-    extra = lax.dot_general(
-        spread_u, adapter_in, (((1,), (1,)), ((), ())), preferred_element_type=jnp.float32
+    extra = lax.optimization_barrier(
+        lax.dot_general(
+            spread_u, adapter_in, (((1,), (1,)), ((), ())), preferred_element_type=jnp.float32
+        )
     )
     base = lax.dot_general(
         full_rows, down_weight, (((1,), (1,)), ((), ())), preferred_element_type=jnp.float32

time: 109 us -> 142 us (1.30)
  the two profiles are of different devices: /device:TPU:0 before, /device:TPU:11 now
where the time goes in v3:
time: 142 us
  waiting for transfers between devices  56.6 us (40%)
  matrix products  36.4 us (26%)
  between operations  14.2 us (10%)
  starting transfers between devices  12.6 us (9%)
  local copies, waits for them, and re-layouts  11.1 us (8%)
  Pallas kernels  9.35 us (7%)
    all_to_all x1, waiting for transfers between devices, sum_blocks(): return jnp.sum(lax.all_to_all(tiled, 'tensor', 0, 0, tiled=True), axis=0)  55.9 us
    dot_general x1, matrix products, per_device(): lax.dot_general(full_rows, down_weight, (((1,), (1,)), ((), ())), preferr...  16.4 us
    pallas_call x1, Pallas kernels, rows_matmul(): pl.pallas_call(_rows_kernel, grid=(m // tile,), in_specs=[pl.BlockSpec((t...  9.35 us
    dot_general x1, matrix products, per_device(): lax.dot_general(spread_u, adapter_in, (((1,), (1,)), ((), ())), preferred...  7.98 us
    dot_general x1, matrix products, per_device(): wide_v = jnp.dot(hidden, adapter_in, preferred_element_type=jnp.float32)  7.69 us
    unnamed x13, local copies, waits for them, and re-layouts  7.23 us
    all_to_all x1, starting transfers between devices, per_device(): lax.all_to_all(pieces, 'tensor', 0, 0, tiled=True)  6.52 us
    all_to_all x1, starting transfers between devices, sum_blocks(): return jnp.sum(lax.all_to_all(tiled, 'tensor', 0, 0, tiled=True), axis=0)  6.02 us
  transfers between devices with their start and end apart: 3, of which 1 were waited for; matrix products, arithmetic and copies ran while one was open for 18% of the time, Pallas kernels for 7%

profile of v3, /device:TPU:11, one launch (start us, length us, event | category | flops | bytes accessed | tf_op | source)
XLA Modules:
  0.0 141.6 jit_solution(836094583761435569)
XLA Ops:
  7.2 0.0 copy-start
  7.2 1.2 copy.31
  8.4 0.8 copy.33
  9.2 6.5 %all-to-all-start = ((bf16[16,12,512]{2,1,0:T(8,128)(2,1)}), bf16[16,12,512]{2,1,0:T(8,128)(2,1)S(1)}, u32[]{:S(2)}, u32[]{:S(2)}) async-start(bf16[16,12,512]{2,1,0:T(8,128)(2,1)} %bitcast.21), calls=%async_computation | async-start | bytes 524288 | tf_op jit(solution)/shard_map/all_to_all | solution.py:78
  15.7 0.0 all-gather.3.cloned.1.call-start
  15.8 0.7 all-gather.3.cloned.1.call-update
  16.5 0.0 copy-start.3
  16.5 0.0 copy-start.4
  16.5 7.7 %fusion.5 = f32[192,2560]{0,1:T(8,128)S(1)} fusion(bf16[192,1792]{1,0:T(8,128)(2,1)} %param.8, bf16[1792,2560]{1,0:T(8,128)(2,1)} %param.10), kind=kOutput, calls=%fused_computation.15 | convolution fusion | flops 1761607680 | bytes 11829248 | tf_op jit(solution)/shard_map/dot_general | solution.py:84
  24.2 0.0 copy-done.3
  24.2 0.0 copy-done.4
  24.2 0.3 broadcast_multiply_fusion
  24.5 0.4 multiply_reduce_fusion
  24.9 0.0 all-to-all-done
  24.9 0.0 copy-done
  24.9 0.9 multiply_reduce_fusion.1
  25.8 0.0 copy-start.2
  25.8 0.1 copy.25
  25.9 1.3 broadcast_in_dim.2
  27.2 6.0 %all-to-all-start.1 = ((f32[16,192,128]{2,1,0:T(8,128)}), f32[16,192,128]{2,1,0:T(8,128)S(1)}, u32[]{:S(2)}, u32[]{:S(2)}) async-start(f32[16,192,128]{2,1,0:T(8,128)} %broadcast_in_dim.2), calls=%async_computation.1 | async-start | bytes 3145728 | tf_op jit(solution)/shard_map/all_to_all | solution.py:64
  33.2 0.0 copy-done.2
  33.2 1.3 copy.27
  34.6 55.9 %all-to-all-done.1 = f32[16,192,128]{2,1,0:T(8,128)S(1)} async-done(((f32[16,192,128]{2,1,0:T(8,128)}), f32[16,192,128]{2,1,0:T(8,128)S(1)}, u32[]{:S(2)}, u32[]{:S(2)}) %all-to-all-start.1) | async-done | bytes 1572896 | tf_op jit(solution)/shard_map/all_to_all | solution.py:64
  90.5 0.1 reduce_sum.29
  90.6 0.1 fusion.4
  90.7 0.1 copy.29
  90.8 0.1 copy.26
  90.9 0.8 multiply_convert_fusion
  91.7 1.4 copy.28.rhs_ref
  93.1 8.0 %fusion.6 = f32[192,1792]{1,0:T(8,128)} fusion(bf16[192,2560]{0,1:T(8,128)(2,1)S(1)} %bitcast.25, bf16[1792,2560]{1,0:T(8,128)(2,1)} %param.10), kind=kOutput, calls=%fused_computation.16 | convolution fusion | flops 1761607680 | bytes 11534336 | tf_op jit(solution)/shard_map/dot_general | solution.py:94
  101.1 9.3 %shard_map.94 = f32[1792,2560]{1,0:T(8,128)} custom-call(bf16[1792,192]{1,0:T(8,128)(2,1)} %bitcast.26, bf16[192,2560]{1,0:T(8,128)(2,1)} %copy.28.rhs_ref), custom_call_target="tpu_custom_call" | custom-call | tf_op jit(solution)/shard_map/pallas_call | solution.py:43
  110.4 3.2 %fusion.7 = f32[2560,512]{1,0:T(8,128)} fusion(bf16[192,2560]{0,1:T(8,128)(2,1)S(1)} %bitcast.23, bf16[192,512]{1,0:T(8,128)(2,1)S(1)} %reshape.44), kind=kOutput, calls=%fused_computation.17 | convolution fusion | flops 503316480 | bytes 6422528 | tf_op jit(solution)/shard_map/dot_general | solution.py:90
  113.6 0.0 all-gather.3.cloned.1.call-done
  113.6 4.7 %reshape.47 = bf16[192,8192]{1,0:T(8,128)(2,1)} reshape(bf16[16,12,8192]{2,1,0:T(8,128)(2,1)} %all-gather.3.cloned.1.call-done) | data formatting | bytes 6291456
  118.3 0.0 copy-start.1
  118.3 16.4 %fusion = bf16[192,1792]{1,0:T(8,128)(2,1)} fusion(f32[192,1792]{1,0:T(8,128)} %fusion.6, bf16[192,8192]{1,0:T(8,128)(2,1)} %reshape.47, bf16[1792,8192]{1,0:T(8,128)(2,1)} %param.9), kind=kOutput, calls=%fused_computation.5 | convolution fusion | flops 5637832704 | bytes 34570240 | tf_op jit(solution)/shard_map/dot_general | solution.py:98
  134.7 0.0 copy-done.1
  (4 shorter events, 0.1 us)
Async XLA Ops:
  7.2 17.8 %copy-start = (bf16[2560,512]{1,0:T(8,128)(2,1)S(1)}, bf16[2560,512]{1,0:T(8,128)(2,1)}, u32[]{:S(2)}) copy-start(bf16[2560,512]{1,0:T(8,128)(2,1)} %param.11) | copy-start | bytes 7864324
  9.2 15.7 %all-to-all-start = ((bf16[16,12,512]{2,1,0:T(8,128)(2,1)}), bf16[16,12,512]{2,1,0:T(8,128)(2,1)S(1)}, u32[]{:S(2)}, u32[]{:S(2)}) async-start(bf16[16,12,512]{2,1,0:T(8,128)(2,1)} %bitcast.21), calls=%async_computation | async-start | bytes 524288 | tf_op jit(solution)/shard_map/all_to_all | solution.py:78
  15.7 97.9 %all-gather.3.cloned.1.call-start = ((), (), s32[]{:S(2)}) async-start(), calls=%async_computation.2 | async-start | bytes 4456448 | tf_op jit(solution)/shard_map/all_gather | solution.py:76
  16.5 7.7 %copy-start.3 = (s32[192]{0:T(256)S(1)}, s32[192]{0:T(256)}, u32[]{:S(2)}) copy-start(s32[192]{0:T(256)} %param.12) | copy-start | bytes 2308
  16.5 7.7 %copy-start.4 = (s32[12]{0:T(128)S(1)}, s32[12]{0:T(128)}, u32[]{:S(2)}) copy-start(s32[12]{0:T(128)} %param.13) | copy-start | bytes 148
  25.8 7.4 %copy-start.2 = (bf16[192,1792]{1,0:T(8,128)(2,1)S(1)}, bf16[192,1792]{1,0:T(8,128)(2,1)}, u32[]{:S(2)}) copy-start(bf16[192,1792]{1,0:T(8,128)(2,1)} %param.8) | copy-start | bytes 2064388
  27.2 63.3 %all-to-all-start.1 = ((f32[16,192,128]{2,1,0:T(8,128)}), f32[16,192,128]{2,1,0:T(8,128)S(1)}, u32[]{:S(2)}, u32[]{:S(2)}) async-start(f32[16,192,128]{2,1,0:T(8,128)} %broadcast_in_dim.2), calls=%async_computation.1 | async-start | bytes 3145728 | tf_op jit(solution)/shard_map/all_to_all | solution.py:64
  118.3 16.4 %copy-start.1 = (bf16[2560,512]{1,0:T(8,128)(2,1)S(1)}, bf16[2560,512]{1,0:T(8,128)(2,1)}, u32[]{:S(2)}) copy-start(bf16[2560,512]{1,0:T(8,128)(2,1)} %param.11) | copy-start | bytes 7864324
Sparse Core Ops, SparseCore 0:
  18.7 67.7 all-gather.2

commit v4 on v3

--- a/solution.py
+++ b/solution.py
@@ -59,9 +59,6 @@
 
 
 def sum_blocks(partial, shards):
-    if shards <= 16:
-        tiled = jnp.broadcast_to(partial[None], (shards,) + partial.shape)
-        return jnp.sum(lax.all_to_all(tiled, "tensor", 0, 0, tiled=True), axis=0)
     rows = partial.shape[0] // shards
     pieces = partial.reshape((shards, rows) + partial.shape[1:])
     got = lax.all_to_all(pieces, "tensor", 0, 0, tiled=True)

time: 142 us -> 109 us (0.77)
  the two profiles are of different devices: /device:TPU:11 before, /device:TPU:0 now
where the time goes in v4:
time: 109 us; the launch traced here: 108 us
  matrix products  36.5 us (33%)
  between operations  14.2 us (13%)
  blocking collectives  12.9 us (12%)
  waiting for transfers between devices  11.4 us (10%)
  local copies, waits for them, and re-layouts  11.3 us (10%)
  starting transfers between devices  11.1 us (10%)
  Pallas kernels  9.35 us (9%)
  other arithmetic  1.26 us (1%)
    dot_general x1, matrix products, per_device(): lax.dot_general(full_rows, down_weight, (((1,), (1,)), ((), ())), preferr...  16.4 us
    all_to_all x1, blocking collectives, sum_blocks(): got = lax.all_to_all(pieces, 'tensor', 0, 0, tiled=True)  12.9 us
    pallas_call x1, Pallas kernels, rows_matmul(): pl.pallas_call(_rows_kernel, grid=(m // tile,), in_specs=[pl.BlockSpec((t...  9.35 us
    unnamed x11, local copies, waits for them, and re-layouts  8.01 us
    all_to_all x1, waiting for transfers between devices, gather_blocks(): got = lax.all_to_all(tiled, 'tensor', 0, 0, tiled=True)  7.97 us
    dot_general x1, matrix products, per_device(): lax.dot_general(spread_u, adapter_in, (((1,), (1,)), ((), ())), preferred...  7.96 us
    dot_general x1, matrix products, per_device(): wide_v = jnp.dot(hidden, adapter_in, preferred_element_type=jnp.float32)  7.84 us
    all_to_all x1, starting transfers between devices, per_device(): lax.all_to_all(pieces, 'tensor', 0, 0, tiled=True)  7.39 us
  transfers between devices with their start and end apart: 3, of which 2 were waited for; matrix products, arithmetic and copies ran while one was open for 26% of the time, Pallas kernels for 9%

profile of v4, /device:TPU:0, one launch (start us, length us, event | category | flops | bytes accessed | tf_op | source)
XLA Modules:
  0.0 108.1 jit_solution(14946416343931061995)
XLA Ops:
  7.2 0.0 copy-start
  7.2 0.0 all-gather.3.cloned.1.call-start
  7.2 0.7 all-gather.3.cloned.1.call-update
  7.9 1.1 copy.28
  9.0 0.8 copy.30
  9.8 7.4 %all-to-all-start = ((bf16[16,12,512]{2,1,0:T(8,128)(2,1)}), bf16[16,12,512]{2,1,0:T(8,128)(2,1)S(1)}, u32[]{:S(2)}, u32[]{:S(2)}) async-start(bf16[16,12,512]{2,1,0:T(8,128)(2,1)} %bitcast.21), calls=%async_computation | async-start | bytes 524288 | tf_op jit(solution)/shard_map/all_to_all | solution.py:75
  17.2 0.0 copy-start.2
  17.2 0.0 copy-start.3
  17.3 7.8 %fusion.5 = f32[192,2560]{0,1:T(8,128)S(1)} fusion(bf16[192,1792]{1,0:T(8,128)(2,1)} %param.8, bf16[1792,2560]{1,0:T(8,128)(2,1)} %param.10), kind=kOutput, calls=%fused_computation.15 | convolution fusion | flops 1761607680 | bytes 11829248 | tf_op jit(solution)/shard_map/dot_general | solution.py:81
  25.1 0.0 copy-done.2
  25.1 0.0 copy-done.3
  25.1 0.3 broadcast_multiply_fusion
  25.4 0.4 multiply_reduce_fusion
  25.8 2.7 %all-to-all-done = bf16[16,12,512]{2,1,0:T(8,128)(2,1)S(1)} async-done(((bf16[16,12,512]{2,1,0:T(8,128)(2,1)}), bf16[16,12,512]{2,1,0:T(8,128)(2,1)S(1)}, u32[]{:S(2)}, u32[]{:S(2)}) %all-to-all-start) | async-done | bytes 196640 | tf_op jit(solution)/shard_map/all_to_all | solution.py:75
  28.6 0.0 copy-done
  28.6 0.9 multiply_reduce_fusion.1
  29.5 0.1 copy.22
  29.6 12.9 %all_to_all.15 = f32[16,12,128]{2,1,0:T(8,128)S(1)} all-to-all(f32[16,12,128]{2,1,0:T(8,128)S(1)} %reshape.52), channel_id=1, replica_groups=mesh['parts'=2,'tensor'=16] {'tensor'}, dimensions={0} | all-to-all | bytes 196608 | tf_op jit(solution)/shard_map/all_to_all | solution.py:64
  42.5 0.7 broadcast_in_dim.2
  43.2 3.7 %all-to-all-start.2 = ((f32[16,12,128]{2,1,0:T(8,128)}), f32[16,12,128]{2,1,0:T(8,128)S(1)}, u32[]{:S(2)}, u32[]{:S(2)}) async-start(f32[16,12,128]{2,1,0:T(8,128)} %broadcast_in_dim.2), calls=%async_computation.2 | async-start | bytes 262144 | tf_op jit(solution)/shard_map/all_to_all | solution.py:57
  46.9 2.2 %copy.24 = bf16[192,1792]{0,1:T(8,128)(2,1)} copy(bf16[192,1792]{1,0:T(8,128)(2,1)} %param.8) | data formatting | bytes 1376256 | tf_op args[1]
  49.1 8.0 %all-to-all-done.2 = f32[16,12,128]{2,1,0:T(8,128)S(1)} async-done(((f32[16,12,128]{2,1,0:T(8,128)}), f32[16,12,128]{2,1,0:T(8,128)S(1)}, u32[]{:S(2)}, u32[]{:S(2)}) %all-to-all-start.2) | async-done | bytes 98336 | tf_op jit(solution)/shard_map/all_to_all | solution.py:57
  57.1 0.1 fusion.4
  57.2 0.1 copy.26
  57.3 0.1 copy.23
  57.4 0.8 multiply_convert_fusion
  58.2 1.4 %copy.25.rhs_ref = bf16[192,2560]{1,0:T(8,128)(2,1)} copy(bf16[192,2560]{0,1:T(8,128)(2,1)S(1)} %bitcast.24) | data formatting | bytes 1966080 | tf_op jit(solution)/shard_map/convert_element_type | solution.py:31
  59.6 8.0 %fusion.6 = f32[192,1792]{1,0:T(8,128)} fusion(bf16[192,2560]{0,1:T(8,128)(2,1)S(1)} %bitcast.25, bf16[1792,2560]{1,0:T(8,128)(2,1)} %param.10), kind=kOutput, calls=%fused_computation.16 | convolution fusion | flops 1761607680 | bytes 11534336 | tf_op jit(solution)/shard_map/dot_general | solution.py:91
  67.5 9.4 %shard_map.94 = f32[1792,2560]{1,0:T(8,128)} custom-call(bf16[1792,192]{1,0:T(8,128)(2,1)} %bitcast.26, bf16[192,2560]{1,0:T(8,128)(2,1)} %copy.25.rhs_ref), custom_call_target="tpu_custom_call" | custom-call | tf_op jit(solution)/shard_map/pallas_call | solution.py:43
  76.9 3.2 %fusion.7 = f32[2560,512]{1,0:T(8,128)} fusion(bf16[192,2560]{0,1:T(8,128)(2,1)S(1)} %bitcast.23, bf16[192,512]{1,0:T(8,128)(2,1)S(1)} %reshape.50), kind=kOutput, calls=%fused_computation.17 | convolution fusion | flops 503316480 | bytes 6422528 | tf_op jit(solution)/shard_map/dot_general | solution.py:87
  80.1 0.0 all-gather.3.cloned.1.call-done
  80.1 4.7 %reshape.55 = bf16[192,8192]{1,0:T(8,128)(2,1)} reshape(bf16[16,12,8192]{2,1,0:T(8,128)(2,1)} %all-gather.3.cloned.1.call-done) | data formatting | bytes 6291456
  84.8 0.0 copy-start.1
  84.8 16.4 %fusion = bf16[192,1792]{1,0:T(8,128)(2,1)} fusion(f32[192,1792]{1,0:T(8,128)} %fusion.6, bf16[192,8192]{1,0:T(8,128)(2,1)} %reshape.55, bf16[1792,8192]{1,0:T(8,128)(2,1)} %param.9), kind=kOutput, calls=%fused_computation.5 | convolution fusion | flops 5637832704 | bytes 34570240 | tf_op jit(solution)/shard_map/dot_general | solution.py:95
  101.2 0.0 copy-done.1
  (7 shorter events, 0.2 us)
Async XLA Ops:
  7.2 21.4 %copy-start = (bf16[2560,512]{1,0:T(8,128)(2,1)S(1)}, bf16[2560,512]{1,0:T(8,128)(2,1)}, u32[]{:S(2)}) copy-start(bf16[2560,512]{1,0:T(8,128)(2,1)} %param.11) | copy-start | bytes 7864324
  7.2 72.9 %all-gather.3.cloned.1.call-start = ((), (), s32[]{:S(2)}) async-start(), calls=%async_computation.3 | async-start | bytes 4456448 | tf_op jit(solution)/shard_map/all_gather | solution.py:73
  9.8 18.7 %all-to-all-start = ((bf16[16,12,512]{2,1,0:T(8,128)(2,1)}), bf16[16,12,512]{2,1,0:T(8,128)(2,1)S(1)}, u32[]{:S(2)}, u32[]{:S(2)}) async-start(bf16[16,12,512]{2,1,0:T(8,128)(2,1)} %bitcast.21), calls=%async_computation | async-start | bytes 524288 | tf_op jit(solution)/shard_map/all_to_all | solution.py:75
  17.2 7.9 %copy-start.2 = (s32[192]{0:T(256)S(1)}, s32[192]{0:T(256)}, u32[]{:S(2)}) copy-start(s32[192]{0:T(256)} %param.12) | copy-start | bytes 2308
  17.2 7.9 %copy-start.3 = (s32[12]{0:T(128)S(1)}, s32[12]{0:T(128)}, u32[]{:S(2)}) copy-start(s32[12]{0:T(128)} %param.13) | copy-start | bytes 148
  43.2 13.9 %all-to-all-start.2 = ((f32[16,12,128]{2,1,0:T(8,128)}), f32[16,12,128]{2,1,0:T(8,128)S(1)}, u32[]{:S(2)}, u32[]{:S(2)}) async-start(f32[16,12,128]{2,1,0:T(8,128)} %broadcast_in_dim.2), calls=%async_computation.2 | async-start | bytes 262144 | tf_op jit(solution)/shard_map/all_to_all | solution.py:57
  84.8 16.4 %copy-start.1 = (bf16[2560,512]{1,0:T(8,128)(2,1)S(1)}, bf16[2560,512]{1,0:T(8,128)(2,1)}, u32[]{:S(2)}) copy-start(bf16[2560,512]{1,0:T(8,128)(2,1)} %param.11) | copy-start | bytes 7864324
Sparse Core Ops, SparseCore 0:
  10.1 56.6 all-gather.2
